TPU v7x, 32 devices: a whole 2x2x4 slice. The times are simulated.
32 devices in a mesh: crop: 1, res: 32 (over z, y, x, core).
Axes of the slice: x: 2, y: 2, z: 4, core: 2. Of those that a mesh axis runs over, the one named last changes fastest.
Arguments:
- homolog_symbol_ids: int32 [64, 128], P(('crop', 'res')), may hold values from 0 to 22
- residue_attend_mask: int32 [128], P('crop'), may hold values 0 or 1
- alignment_state: bfloat16 [64, 128, 256], P(('crop', 'res')), may hold values from -6 to 6
- pair: bfloat16 [128, 128, 128], P(('crop', 'res')), may hold values from -6 to 6
- symbol_lookup_matrix: bfloat16 [23, 256], replicated, may hold values from -3 to 3
- pair_bias_weight: bfloat16 [128, 8], replicated, may hold values from -0.5 to 0.5
- row_projection_weight: bfloat16 [256, 1024], replicated, may hold values from -8 to 8
- horizontal_readout_matrix: bfloat16 [256, 256], replicated, may hold values from -0.375 to 0.375
- column_projection_weight: bfloat16 [256, 1024], replicated, may hold values from -8 to 8
- vertical_readout_matrix: bfloat16 [256, 256], replicated, may hold values from -0.375 to 0.375
- product_factor_matrices: bfloat16 [256, 64], replicated, may hold values from -0.375 to 0.375
- outer_output_weight: bfloat16 [1024, 128], replicated, may hold values from -1.5 to 1.5
- triangle_input_weight: bfloat16 [128, 640], replicated, may hold values from -0.5 to 0.5
- triangle_output_weight: bfloat16 [128, 128], replicated, may hold values from -0.5 to 0.5
Outputs:
- alignment_output: bfloat16 [64, 128, 256], P('crop', 'res')
- pair_output: bfloat16 [128, 128, 128], P(('crop', 'res'))
All inputs are finite; a program needn't handle non-finite values.
Results may differ from a plain program's by a relative error of at most 0.013.
Values may be sent and summed in bfloat16 or wider, within the bound.
A program may use at most 64 MiB of HBM per device.

v0:
```python
import jax
import jax.numpy as jnp
from jax import lax
from jax.sharding import PartitionSpec as P

EPSILON = 1e-05


def layer_normalized(input_rows, axis):
    average = jnp.mean(input_rows, axis, keepdims=True)
    centred = input_rows - average
    spread = jnp.mean(centred * centred, axis, keepdims=True)
    return centred * lax.rsqrt(spread + EPSILON)


def split_proj(input_rows, weight, head_count):
    channels = weight.shape[0]
    head_size = channels // head_count
    projected = jnp.einsum("blc,ce->ble", input_rows, weight, preferred_element_type=jnp.float32)
    lead = projected.shape[:2]
    query_tensor = (
        (projected[..., :channels] * head_size ** (-0.5))
        .astype(jnp.bfloat16)
        .reshape(lead + (head_count, head_size))
    )
    key_tensor = (
        projected[..., channels : 2 * channels]
        .astype(jnp.bfloat16)
        .reshape(lead + (head_count, head_size))
    )
    value_tensor = (
        projected[..., 2 * channels : 3 * channels]
        .astype(jnp.bfloat16)
        .reshape(lead + (head_count, head_size))
    )
    gate_values = projected[..., 3 * channels :]
    return (query_tensor, key_tensor, value_tensor, gate_values)


def attention_block_fn(query_tensor, key_tensor, value_tensor, gate_values, extra_bias, out_weight):
    scores = (
        jnp.einsum("bqhd,bkhd->bhqk", query_tensor, key_tensor, preferred_element_type=jnp.float32)
        + extra_bias
    )
    row_top = jnp.max(scores, -1, keepdims=True)
    exp_scores = jnp.exp(scores - row_top)
    weights = (exp_scores / jnp.sum(exp_scores, -1, keepdims=True)).astype(jnp.bfloat16)
    mixed = jnp.einsum("bhqk,bkhd->bqhd", weights, value_tensor, preferred_element_type=jnp.float32)
    gated = (jax.nn.sigmoid(gate_values) * mixed.reshape(gate_values.shape)).astype(jnp.bfloat16)
    return jnp.einsum("bqc,ce->bqe", gated, out_weight, preferred_element_type=jnp.float32)


def shards(
    homolog_symbol_ids,
    residue_attend_mask,
    alignment_state,
    pair,
    symbol_lookup_matrix,
    pair_bias_weight,
    row_projection_weight,
    horizontal_readout_matrix,
    column_projection_weight,
    vertical_readout_matrix,
    product_factor_matrices,
    outer_output_weight,
    triangle_input_weight,
    triangle_output_weight,
):
    residue_count = lax.axis_size("res")
    sequence_total = alignment_state.shape[0] * residue_count
    res_local = pair.shape[0]
    chain_total = pair.shape[1]
    pair_chan = pair.shape[2]
    owner_chan = pair_chan // residue_count
    outer_chan = product_factor_matrices.shape[1] // 2
    head_count = pair_bias_weight.shape[1]
    token_class_count = symbol_lookup_matrix.shape[0]
    one_hot_tokens = (
        homolog_symbol_ids[:, :, None]
        == jnp.arange(token_class_count, dtype=jnp.int32)[None, None, :]
    ).astype(jnp.bfloat16)
    alignment_initial = alignment_state.astype(jnp.float32) + jnp.einsum(
        "kly,yb->klb", one_hot_tokens, symbol_lookup_matrix, preferred_element_type=jnp.float32
    )
    pair_normed = layer_normalized(pair.astype(jnp.float32), -1).astype(jnp.bfloat16)
    bias_local = jnp.einsum(
        "ijc,ch->hij", pair_normed, pair_bias_weight, preferred_element_type=jnp.float32
    ).astype(jnp.bfloat16)
    mask_bias = (residue_attend_mask.astype(jnp.float32) - 1.0) * 10000.0
    row_input = layer_normalized(alignment_initial, -1).astype(jnp.bfloat16)
    query_tensor, key_tensor, value_tensor, gate_values = split_proj(
        row_input, row_projection_weight, head_count
    )
    bias_all = lax.all_gather(bias_local, "res", axis=1, tiled=True)
    extra_bias = bias_all.astype(jnp.float32)[None] + mask_bias[None, None, None, :]
    row_attention_update = attention_block_fn(
        query_tensor, key_tensor, value_tensor, gate_values, extra_bias, horizontal_readout_matrix
    )
    alignment_after_rows = (alignment_initial + row_attention_update).astype(jnp.bfloat16)
    alignment_columns = lax.all_to_all(
        alignment_after_rows, "res", split_axis=1, concat_axis=0, tiled=True
    )
    column_start = jnp.swapaxes(alignment_columns, 0, 1).astype(jnp.float32)
    col_in = layer_normalized(column_start, -1).astype(jnp.bfloat16)
    col_queries, col_keys, col_values, col_gating = split_proj(
        col_in, column_projection_weight, head_count
    )
    alignment_after_columns = column_start + attention_block_fn(
        col_queries, col_keys, col_values, col_gating, jnp.float32(0.0), vertical_readout_matrix
    )
    alignment_output = jnp.swapaxes(alignment_after_columns, 0, 1).astype(jnp.bfloat16)
    outer_input = layer_normalized(alignment_after_columns, -1).astype(jnp.bfloat16)
    factor_ab = jnp.einsum(
        "rsc,ce->rse", outer_input, product_factor_matrices, preferred_element_type=jnp.float32
    )
    left = factor_ab[..., :outer_chan].astype(jnp.bfloat16)
    latter_factor = (
        factor_ab[..., outer_chan:]
        .astype(jnp.bfloat16)
        .reshape(res_local, sequence_total * outer_chan)
    )
    piece = lax.all_gather(latter_factor, "res", axis=0, tiled=True)
    count = piece.shape[0]
    right_rows = piece.reshape(count, sequence_total, outer_chan)
    cross_product_result = (
        jnp.einsum("isc,jsd->ijcd", left, right_rows, preferred_element_type=jnp.float32)
        / sequence_total
    ).astype(jnp.bfloat16)
    update = jnp.einsum(
        "ije,ez->ijz",
        cross_product_result.reshape(res_local, count, outer_chan * outer_chan),
        outer_output_weight,
        preferred_element_type=jnp.float32,
    )
    pair_one = pair.astype(jnp.float32) + update
    tri_normed = layer_normalized(pair_one, -1).astype(jnp.bfloat16)
    factors = jnp.einsum(
        "ijc,ce->eij",
        tri_normed,
        triangle_input_weight[:, : 4 * pair_chan],
        preferred_element_type=jnp.float32,
    )
    gate_out = jnp.einsum(
        "ijc,ce->ije",
        tri_normed,
        triangle_input_weight[:, 4 * pair_chan :],
        preferred_element_type=jnp.float32,
    )
    left_f = (jax.nn.sigmoid(factors[pair_chan : 2 * pair_chan]) * factors[:pair_chan]).astype(
        jnp.bfloat16
    )
    right_f = (
        jax.nn.sigmoid(factors[3 * pair_chan :]) * factors[2 * pair_chan : 3 * pair_chan]
    ).astype(jnp.bfloat16)
    left_f = left_f.reshape(residue_count, owner_chan, res_local, chain_total)
    right_f = right_f.reshape(residue_count, owner_chan, res_local, chain_total)
    combined = jnp.einsum(
        "xcik,xcjk->xcij",
        lax.all_to_all(left_f, "res", split_axis=0, concat_axis=2, tiled=True),
        lax.all_to_all(right_f, "res", split_axis=0, concat_axis=2, tiled=True),
        preferred_element_type=jnp.float32,
    ).astype(jnp.bfloat16)
    back_rows = lax.all_to_all(combined, "res", split_axis=2, concat_axis=0, tiled=True)
    back_rows = back_rows.reshape(pair_chan, res_local, chain_total)
    comb_normed = layer_normalized(back_rows.astype(jnp.float32), 0).astype(jnp.bfloat16)
    tri_update = jnp.einsum(
        "cij,cz->ijz", comb_normed, triangle_output_weight, preferred_element_type=jnp.float32
    )
    pair_output = (pair_one + jax.nn.sigmoid(gate_out) * tri_update).astype(jnp.bfloat16)
    return (alignment_output, pair_output)


def solution(mesh):
    placed = (
        P(("crop", "res"), None),
        P("crop"),
        P(("crop", "res"), None, None),
        P(("crop", "res"), None, None),
        P(),
        P(),
        P(),
        P(),
        P(),
        P(),
        P(),
        P(),
        P(),
        P(),
    )
    return jax.shard_map(
        shards,
        mesh=mesh,
        in_specs=placed,
        out_specs=(P("crop", "res", None), P(("crop", "res"), None, None)),
        check_vma=False,
    )
```

profile of v0, /device:TPU:0, one launch (start us, length us, event | category | flops | bytes accessed | tf_op | source)
XLA Modules:
  0.0 155.3 jit_solution(11216174859262117624)
XLA Ops:
  0.7 0.7 add_multiply_fusion
  1.4 1.0 copy.74
  2.5 0.8 fusion.14
  3.4 43.9 %all_gather.6 = bf16[8,128,128]{2,0,1:T(8,128)(2,1)S(1)} all-gather(bf16[8,4,128]{2,0,1:T(8,128)(2,1)S(1)} %fusion.14), channel_id=1, replica_groups=mesh['crop'=1,'res'=32] {'res'}, dimensions={1}, use_global_device_ids=true | all-gather | bytes 270336 | tf_op jit(solution)/shard_map/all_gather | solution.py:94
  47.3 0.2 copy.76
  47.6 0.3 fusion.84
  47.9 0.2 multiply_reduce_fusion.3
  48.1 0.3 fusion.85
  48.5 0.7 fusion.83
  49.2 0.1 copy.73
  49.3 0.1 copy.72
  49.5 0.5 copy-done.1
  49.9 0.2 copy-done.2
  50.1 0.5 fusion.86
  50.6 1.3 convolution_add_fusion
  51.9 1.0 copy.71
  53.0 1.0 fusion.20
  54.0 1.1 copy.78
  55.2 1.1 fusion.11
  56.3 0.1 copy.79
  56.4 9.9 %all_to_all.48 = bf16[2,128,256]{2,0,1:T(2,128)(2,1)S(1)} all-to-all(bf16[2,128,256]{2,0,1:T(2,128)(2,1)S(1)} %copy.79), channel_id=1, replica_groups=mesh['crop'=1,'res'=32] {'res'}, dimensions={1} | all-to-all | bytes 262144 | tf_op jit(solution)/shard_map/all_to_all | solution.py:100
  66.4 0.2 reshape.167
  66.6 0.1 bitcast_reduce_fusion.1
  66.7 0.2 multiply_reduce_fusion.2
  66.9 0.3 fusion.87
  67.3 0.7 fusion.82
  68.0 0.2 copy.83
  68.2 0.2 copy.82
  68.4 0.5 fusion.88
  68.9 0.3 fusion.90
  69.2 1.1 copy.81
  70.3 1.2 fusion.19
  71.4 1.2 copy.85
  72.7 1.1 fusion.46
  73.8 0.1 fusion.81
  73.9 0.2 multiply_reduce_fusion.1
  74.1 0.3 convolution_convert_fusion.1
  74.4 0.1 copy.86
  74.5 0.1 reshape.173
  74.7 39.3 %all-gather = bf16[32,4,2048]{2,1,0:T(4,128)(2,1)S(1)} all-gather(bf16[1,4,2048]{2,1,0:T(4,128)(2,1)S(1)} %reshape.173), channel_id=1, replica_groups=mesh['crop'=1,'res'=32] {'res'}, dimensions={0}, use_global_device_ids=true | all-gather | bytes 540672 | tf_op jit(solution)/shard_map/all_gather | solution.py:122
  114.0 1.2 reshape.160
  115.2 2.6 %copy.109 = bf16[128,64,32,1]{0,1,3,2:T(8,128)(2,1)S(1)} copy(bf16[128,64,32,1]{2,1,0,3:T(8,128)(2,1)S(1)} %bitcast.133) | data formatting | bytes 1048576 | tf_op jit(solution)/shard_map/reshape | solution.py:124
  117.8 0.4 fusion.6
  118.2 0.7 copy.88
  118.9 0.4 fusion.89
  119.4 0.3 convolution_bitcast_fusion
  119.7 0.1 fusion.25
  119.8 0.1 copy.97
  120.0 0.7 copy.98
  120.7 2.6 %all-to-all-start.2 = ((bf16[32,4,4,128]{3,1,2,0:T(4,128)(2,1)}), bf16[32,4,4,128]{3,1,2,0:T(4,128)(2,1)S(1)}, u32[]{:S(2)}, u32[]{:S(2)}) async-start(bf16[32,4,4,128]{3,1,2,0:T(4,128)(2,1)} %copy.98), calls=%async_computation.2 | async-start | bytes 262144 | tf_op jit(solution)/shard_map/all_to_all | solution.py:160
  123.3 0.1 copy.94
  123.4 0.7 copy.95
  124.1 7.4 %all-to-all-done.2 = bf16[32,4,4,128]{3,1,2,0:T(4,128)(2,1)S(1)} async-done(((bf16[32,4,4,128]{3,1,2,0:T(4,128)(2,1)}), bf16[32,4,4,128]{3,1,2,0:T(4,128)(2,1)S(1)}, u32[]{:S(2)}, u32[]{:S(2)}) %all-to-all-start.2) | async-done | bytes 131104 | tf_op jit(solution)/shard_map/all_to_all | solution.py:160
  131.5 2.6 %all-to-all-start.1 = ((bf16[32,4,4,128]{3,1,2,0:T(4,128)(2,1)}), bf16[32,4,4,128]{3,1,2,0:T(4,128)(2,1)S(1)}, u32[]{:S(2)}, u32[]{:S(2)}) async-start(bf16[32,4,4,128]{3,1,2,0:T(4,128)(2,1)} %copy.95), calls=%async_computation.1 | async-start | bytes 262144 | tf_op jit(solution)/shard_map/all_to_all | solution.py:159
  134.1 8.1 %all-to-all-done.1 = bf16[32,4,4,128]{3,1,2,0:T(4,128)(2,1)S(1)} async-done(((bf16[32,4,4,128]{3,1,2,0:T(4,128)(2,1)}), bf16[32,4,4,128]{3,1,2,0:T(4,128)(2,1)S(1)}, u32[]{:S(2)}, u32[]{:S(2)}) %all-to-all-start.1) | async-done | bytes 131104 | tf_op jit(solution)/shard_map/all_to_all | solution.py:159
  142.3 0.2 fusion.13
  142.5 0.8 copy.100
  143.3 2.6 %all-to-all-start.3 = ((bf16[1,4,128,128]{3,1,0,2:T(4,128)(2,1)}), bf16[1,4,128,128]{3,1,0,2:T(4,128)(2,1)S(1)}, u32[]{:S(2)}, u32[]{:S(2)}) async-start(bf16[1,4,128,128]{3,1,0,2:T(4,128)(2,1)} %copy.100), calls=%async_computation.3 | async-start | bytes 262144 | tf_op jit(solution)/shard_map/all_to_all | solution.py:163
  145.9 0.8 copy.104
  146.6 0.3 fusion.10
  146.9 7.2 %all-to-all-done.3 = bf16[1,4,128,128]{3,1,0,2:T(4,128)(2,1)S(1)} async-done(((bf16[1,4,128,128]{3,1,0,2:T(4,128)(2,1)}), bf16[1,4,128,128]{3,1,0,2:T(4,128)(2,1)S(1)}, u32[]{:S(2)}, u32[]{:S(2)}) %all-to-all-start.3) | async-done | bytes 131104 | tf_op jit(solution)/shard_map/all_to_all | solution.py:163
  154.2 0.1 fusion.44
  154.3 0.2 fusion.12
  154.6 0.8 copy.105
  (44 shorter events, 0.6 us)
Async XLA Ops:
  0.6 47.5 %copy-start = (bf16[256,1024]{1,0:T(8,128)(2,1)S(1)}, bf16[256,1024]{1,0:T(8,128)(2,1)}, u32[]{:S(2)}) copy-start(bf16[256,1024]{1,0:T(8,128)(2,1)} %param.20) | copy-start | bytes 1572868
  0.6 46.9 %copy-start.9 = (bf16[23,256]{1,0:T(8,128)(2,1)S(1)}, bf16[23,256]{1,0:T(8,128)(2,1)}, u32[]{:S(2)}) copy-start(bf16[23,256]{1,0:T(8,128)(2,1)} %param.18) | copy-start | bytes 35332
  0.7 46.9 %copy-start.5 = (bf16[2,128,256]{2,1,0:T(8,128)(2,1)S(1)}, bf16[2,128,256]{2,1,0:T(8,128)(2,1)}, u32[]{:S(2)}) copy-start(bf16[2,128,256]{2,1,0:T(8,128)(2,1)} %param.16) | copy-start | bytes 393220
  0.7 46.9 %copy-start.10 = (s32[2,128]{1,0:T(2,128)S(1)}, s32[2,128]{1,0:T(2,128)}, u32[]{:S(2)}) copy-start(s32[2,128]{1,0:T(2,128)} %param.14) | copy-start | bytes 3076
  49.3 0.6 copy-start.1
  49.5 0.7 copy-start.2
  54.0 12.9 %copy-start.3 = (bf16[256,1024]{1,0:T(8,128)(2,1)S(1)}, bf16[256,1024]{1,0:T(8,128)(2,1)}, u32[]{:S(2)}) copy-start(bf16[256,1024]{1,0:T(8,128)(2,1)} %param.22) | copy-start | bytes 1572868
  71.4 2.7 %copy-start.7 = (bf16[256,64]{0,1:T(8,128)(2,1)S(1)}, bf16[256,64]{0,1:T(8,128)(2,1)}, u32[]{:S(2)}) copy-start(bf16[256,64]{0,1:T(8,128)(2,1)} %param.24) | copy-start | bytes 98308
  117.8 1.1 copy-start.4
  118.2 1.1 copy-start.6
  120.7 10.8 %all-to-all-start.2 = ((bf16[32,4,4,128]{3,1,2,0:T(4,128)(2,1)}), bf16[32,4,4,128]{3,1,2,0:T(4,128)(2,1)S(1)}, u32[]{:S(2)}, u32[]{:S(2)}) async-start(bf16[32,4,4,128]{3,1,2,0:T(4,128)(2,1)} %copy.98), calls=%async_computation.2 | async-start | bytes 262144 | tf_op jit(solution)/shard_map/all_to_all | solution.py:160
  123.4 30.9 %copy-start.8 = (bf16[128,128]{1,0:T(8,128)(2,1)S(1)}, bf16[128,128]{1,0:T(8,128)(2,1)}, u32[]{:S(2)}) copy-start(bf16[128,128]{1,0:T(8,128)(2,1)} %param.27) | copy-start | bytes 98308
  131.5 10.8 %all-to-all-start.1 = ((bf16[32,4,4,128]{3,1,2,0:T(4,128)(2,1)}), bf16[32,4,4,128]{3,1,2,0:T(4,128)(2,1)S(1)}, u32[]{:S(2)}, u32[]{:S(2)}) async-start(bf16[32,4,4,128]{3,1,2,0:T(4,128)(2,1)} %copy.95), calls=%async_computation.1 | async-start | bytes 262144 | tf_op jit(solution)/shard_map/all_to_all | solution.py:159
  143.3 10.8 %all-to-all-start.3 = ((bf16[1,4,128,128]{3,1,0,2:T(4,128)(2,1)}), bf16[1,4,128,128]{3,1,0,2:T(4,128)(2,1)S(1)}, u32[]{:S(2)}, u32[]{:S(2)}) async-start(bf16[1,4,128,128]{3,1,0,2:T(4,128)(2,1)} %copy.100), calls=%async_computation.3 | async-start | bytes 262144 | tf_op jit(solution)/shard_map/all_to_all | solution.py:163
where the time goes:
time: 156 us; the launch traced here: 155 us
  blocking collectives  93.2 us (60%)
  waiting for transfers between devices  22.7 us (15%)
  local copies, waits for them, and re-layouts  17.4 us (11%)
  matrix products  11 us (7%)
  starting transfers between devices  7.73 us (5%)
  other arithmetic  2.2 us (1%)
    all_gather x1, blocking collectives, shards(): bias_all = lax.all_gather(bias_local, 'res', axis=1, tiled=True)  43.9 us
    all_gather x1, blocking collectives, shards(): piece = lax.all_gather(latter_factor, 'res', axis=0, tiled=True)  39.3 us
    all_to_all x1, blocking collectives, shards(): lax.all_to_all(alignment_after_rows, 'res', split_axis=1, concat_axis=0,...  9.91 us
    all_to_all x1, waiting for transfers between devices, shards(): lax.all_to_all(left_f, 'res', split_axis=0, concat_axis=2, tiled=True)  8.14 us
    all_to_all x1, waiting for transfers between devices, shards(): lax.all_to_all(right_f, 'res', split_axis=0, concat_axis=2, tiled=True)  7.35 us
    all_to_all x1, waiting for transfers between devices, shards(): lax.all_to_all(combined, 'res', split_axis=2, concat_axis=0, tiled=True)  7.17 us
    reshape x2, local copies, waits for them, and re-layouts, shards(): right_rows = piece.reshape(count, sequence_total, outer_chan)  3.78 us
    unnamed x26, local copies, waits for them, and re-layouts  3.38 us
  transfers between devices with their start and end apart: 3, of which 3 were waited for; matrix products, arithmetic and copies ran while one was open for 1% of the time, Pallas kernels for 0%

commit v1 on v0

--- a/solution.py
+++ b/solution.py
@@ -160,7 +160,9 @@
         lax.all_to_all(right_f, "res", split_axis=0, concat_axis=2, tiled=True),
         preferred_element_type=jnp.float32,
     ).astype(jnp.bfloat16)
-    back_rows = lax.all_to_all(combined, "res", split_axis=2, concat_axis=0, tiled=True)
+    m_next = jnp.stack(jnp.split(combined, jax.lax.axis_size("res"), axis=2))
+    outcome_arr = jax.lax.all_to_all(m_next, "res", 0, 0)
+    back_rows = jnp.concatenate(outcome_arr, axis=0)
     back_rows = back_rows.reshape(pair_chan, res_local, chain_total)
     comb_normed = layer_normalized(back_rows.astype(jnp.float32), 0).astype(jnp.bfloat16)
     tri_update = jnp.einsum(

time: 156 us -> 175 us (1.12)
  local copies, waits for them, and re-layouts: 17.4 us -> 35.9 us
    unnamed x26 -> x57, local copies, waits for them, and re-layouts: 3.38 us -> 21.9 us
where the time goes in v1:
time: 175 us; the launch traced here: 174 us
  blocking collectives  93.2 us (53%)
  local copies, waits for them, and re-layouts  35.9 us (21%)
  waiting for transfers between devices  22.7 us (13%)
  matrix products  11.1 us (6%)
  starting transfers between devices  7.73 us (4%)
  other arithmetic  2.32 us (1%)
    all_gather x1, blocking collectives, shards(): bias_all = lax.all_gather(bias_local, 'res', axis=1, tiled=True)  43.9 us
    all_gather x1, blocking collectives, shards(): piece = lax.all_gather(latter_factor, 'res', axis=0, tiled=True)  39.3 us
    unnamed x57, local copies, waits for them, and re-layouts  21.9 us
    all_to_all x1, blocking collectives, shards(): lax.all_to_all(alignment_after_rows, 'res', split_axis=1, concat_axis=0,...  9.91 us
    all_to_all x1, waiting for transfers between devices, shards(): lax.all_to_all(left_f, 'res', split_axis=0, concat_axis=2, tiled=True)  8.14 us
    all_to_all x1, waiting for transfers between devices, shards(): lax.all_to_all(right_f, 'res', split_axis=0, concat_axis=2, tiled=True)  7.35 us
    all_to_all x1, waiting for transfers between devices, shards(): outcome_arr = jax.lax.all_to_all(m_next, 'res', 0, 0)  7.17 us
    reshape x2, local copies, waits for them, and re-layouts, shards(): right_rows = piece.reshape(count, sequence_total, outer_chan)  3.78 us
  transfers between devices with their start and end apart: 3, of which 3 were waited for; matrix products, arithmetic and copies ran while one was open for 1% of the time, Pallas kernels for 0%

profile of v1, /device:TPU:0, one launch (start us, length us, event | category | flops | bytes accessed | tf_op | source)
XLA Modules:
  0.0 174.1 jit_solution(11891882801990096274)
XLA Ops:
  0.7 0.7 add_multiply_fusion
  1.4 1.0 copy.73
  2.5 0.8 fusion.14
  3.4 43.9 %all_gather.6 = bf16[8,128,128]{2,0,1:T(8,128)(2,1)S(1)} all-gather(bf16[8,4,128]{2,0,1:T(8,128)(2,1)S(1)} %fusion.14), channel_id=1, replica_groups=mesh['crop'=1,'res'=32] {'res'}, dimensions={1}, use_global_device_ids=true | all-gather | bytes 270336 | tf_op jit(solution)/shard_map/all_gather | solution.py:94
  48.5 0.7 fusion.81
  50.1 0.5 fusion.84
  50.6 1.3 convolution_add_fusion
  51.9 1.0 copy.70
  53.0 1.0 fusion.20
  54.0 1.1 copy.77
  55.2 1.1 fusion.11
  56.4 9.9 %all_to_all.44 = bf16[2,128,256]{2,0,1:T(2,128)(2,1)S(1)} all-to-all(bf16[2,128,256]{2,0,1:T(2,128)(2,1)S(1)} %copy.78), channel_id=1, replica_groups=mesh['crop'=1,'res'=32] {'res'}, dimensions={1} | all-to-all | bytes 262144 | tf_op jit(solution)/shard_map/all_to_all | solution.py:100
  67.3 0.7 fusion.80
  68.4 0.5 fusion.86
  69.2 1.1 copy.80
  70.3 1.2 fusion.19
  71.4 1.2 copy.84
  72.7 1.1 fusion.44
  74.7 39.3 %all-gather = bf16[32,4,2048]{2,1,0:T(4,128)(2,1)S(1)} all-gather(bf16[1,4,2048]{2,1,0:T(4,128)(2,1)S(1)} %reshape.165), channel_id=1, replica_groups=mesh['crop'=1,'res'=32] {'res'}, dimensions={0}, use_global_device_ids=true | all-gather | bytes 540672 | tf_op jit(solution)/shard_map/all_gather | solution.py:122
  114.0 1.2 reshape.154
  115.2 2.6 %copy.106 = bf16[128,64,32,1]{0,1,3,2:T(8,128)(2,1)S(1)} copy(bf16[128,64,32,1]{2,1,0,3:T(8,128)(2,1)S(1)} %bitcast.252) | data formatting | bytes 1048576 | tf_op jit(solution)/shard_map/reshape | solution.py:124
  118.2 0.7 copy.87
  120.0 0.7 copy.97
  120.7 2.6 %all-to-all-start.2 = ((bf16[32,4,4,128]{3,1,2,0:T(4,128)(2,1)}), bf16[32,4,4,128]{3,1,2,0:T(4,128)(2,1)S(1)}, u32[]{:S(2)}, u32[]{:S(2)}) async-start(bf16[32,4,4,128]{3,1,2,0:T(4,128)(2,1)} %copy.97), calls=%async_computation.2 | async-start | bytes 262144 | tf_op jit(solution)/shard_map/all_to_all | solution.py:160
  123.4 0.7 copy.94
  124.1 7.4 %all-to-all-done.2 = bf16[32,4,4,128]{3,1,2,0:T(4,128)(2,1)S(1)} async-done(((bf16[32,4,4,128]{3,1,2,0:T(4,128)(2,1)}), bf16[32,4,4,128]{3,1,2,0:T(4,128)(2,1)S(1)}, u32[]{:S(2)}, u32[]{:S(2)}) %all-to-all-start.2) | async-done | bytes 131104 | tf_op jit(solution)/shard_map/all_to_all | solution.py:160
  131.5 2.6 %all-to-all-start.1 = ((bf16[32,4,4,128]{3,1,2,0:T(4,128)(2,1)}), bf16[32,4,4,128]{3,1,2,0:T(4,128)(2,1)S(1)}, u32[]{:S(2)}, u32[]{:S(2)}) async-start(bf16[32,4,4,128]{3,1,2,0:T(4,128)(2,1)} %copy.94), calls=%async_computation.1 | async-start | bytes 262144 | tf_op jit(solution)/shard_map/all_to_all | solution.py:159
  134.1 8.1 %all-to-all-done.1 = bf16[32,4,4,128]{3,1,2,0:T(4,128)(2,1)S(1)} async-done(((bf16[32,4,4,128]{3,1,2,0:T(4,128)(2,1)}), bf16[32,4,4,128]{3,1,2,0:T(4,128)(2,1)S(1)}, u32[]{:S(2)}, u32[]{:S(2)}) %all-to-all-start.1) | async-done | bytes 131104 | tf_op jit(solution)/shard_map/all_to_all | solution.py:159
  142.5 0.6 constant_dynamic-update-slice_fusion.31
  143.1 0.6 constant_dynamic-update-slice_fusion.30
  143.7 0.6 constant_dynamic-update-slice_fusion.29
  144.3 0.6 constant_dynamic-update-slice_fusion.28
  144.9 0.6 constant_dynamic-update-slice_fusion.27
  145.5 0.6 constant_dynamic-update-slice_fusion.26
  146.1 0.6 constant_dynamic-update-slice_fusion.25
  146.7 0.6 constant_dynamic-update-slice_fusion.24
  147.3 0.6 constant_dynamic-update-slice_fusion.23
  147.9 0.6 constant_dynamic-update-slice_fusion.22
  148.5 0.6 constant_dynamic-update-slice_fusion.21
  149.1 0.6 constant_dynamic-update-slice_fusion.20
  149.7 0.6 constant_dynamic-update-slice_fusion.19
  150.3 0.6 constant_dynamic-update-slice_fusion.18
  150.9 0.6 constant_dynamic-update-slice_fusion.17
  151.5 0.6 constant_dynamic-update-slice_fusion.16
  152.1 0.6 constant_dynamic-update-slice_fusion.15
  152.7 0.6 constant_dynamic-update-slice_fusion.14
  153.3 0.6 constant_dynamic-update-slice_fusion.13
  153.9 0.6 constant_dynamic-update-slice_fusion.12
  154.5 0.6 constant_dynamic-update-slice_fusion.11
  155.1 0.6 constant_dynamic-update-slice_fusion.10
  155.7 0.6 constant_dynamic-update-slice_fusion.9
  156.3 0.6 constant_dynamic-update-slice_fusion.8
  156.9 0.6 constant_dynamic-update-slice_fusion.7
  157.5 0.6 constant_dynamic-update-slice_fusion.6
  158.1 0.6 constant_dynamic-update-slice_fusion.5
  158.7 0.6 constant_dynamic-update-slice_fusion.4
  159.3 0.6 constant_dynamic-update-slice_fusion.3
  159.9 0.6 constant_dynamic-update-slice_fusion.2
  160.5 0.6 constant_dynamic-update-slice_fusion.1
  161.1 0.6 constant_dynamic-update-slice_fusion
  161.7 2.6 %all-to-all-start.3 = ((bf16[32,1,4,4,128]{4,3,2,1,0:T(4,128)(2,1)}), bf16[32,1,4,4,128]{4,3,2,1,0:T(4,128)(2,1)S(1)}, u32[]{:S(2)}, u32[]{:S(2)}) async-start(bf16[32,1,4,4,128]{4,3,2,1,0:T(4,128)(2,1)} %constant_dynamic-update-slice_fusion), calls=%async_computation.3 | async-start | bytes 262144 | tf_op jit(solution)/shard_map/all_to_all | solution.py:164
  164.3 0.8 copy.101
  165.3 7.2 %all-to-all-done.3 = bf16[32,1,4,4,128]{4,3,2,1,0:T(4,128)(2,1)S(1)} async-done(((bf16[32,1,4,4,128]{4,3,2,1,0:T(4,128)(2,1)}), bf16[32,1,4,4,128]{4,3,2,1,0:T(4,128)(2,1)S(1)}, u32[]{:S(2)}, u32[]{:S(2)}) %all-to-all-start.3) | async-done | bytes 131104 | tf_op jit(solution)/shard_map/all_to_all | solution.py:164
  173.3 0.8 copy.102
  (75 shorter events, 7.7 us)
Async XLA Ops:
  0.6 47.5 %copy-start = (bf16[256,1024]{1,0:T(8,128)(2,1)S(1)}, bf16[256,1024]{1,0:T(8,128)(2,1)}, u32[]{:S(2)}) copy-start(bf16[256,1024]{1,0:T(8,128)(2,1)} %param.20) | copy-start | bytes 1572868
  0.6 46.9 %copy-start.9 = (bf16[23,256]{1,0:T(8,128)(2,1)S(1)}, bf16[23,256]{1,0:T(8,128)(2,1)}, u32[]{:S(2)}) copy-start(bf16[23,256]{1,0:T(8,128)(2,1)} %param.18) | copy-start | bytes 35332
  0.7 46.9 %copy-start.5 = (bf16[2,128,256]{2,1,0:T(8,128)(2,1)S(1)}, bf16[2,128,256]{2,1,0:T(8,128)(2,1)}, u32[]{:S(2)}) copy-start(bf16[2,128,256]{2,1,0:T(8,128)(2,1)} %param.16) | copy-start | bytes 393220
  0.7 46.9 %copy-start.10 = (s32[2,128]{1,0:T(2,128)S(1)}, s32[2,128]{1,0:T(2,128)}, u32[]{:S(2)}) copy-start(s32[2,128]{1,0:T(2,128)} %param.14) | copy-start | bytes 3076
  49.3 0.6 copy-start.1
  49.5 0.7 copy-start.2
  54.0 12.9 %copy-start.3 = (bf16[256,1024]{1,0:T(8,128)(2,1)S(1)}, bf16[256,1024]{1,0:T(8,128)(2,1)}, u32[]{:S(2)}) copy-start(bf16[256,1024]{1,0:T(8,128)(2,1)} %param.22) | copy-start | bytes 1572868
  71.4 2.7 %copy-start.7 = (bf16[256,64]{0,1:T(8,128)(2,1)S(1)}, bf16[256,64]{0,1:T(8,128)(2,1)}, u32[]{:S(2)}) copy-start(bf16[256,64]{0,1:T(8,128)(2,1)} %param.24) | copy-start | bytes 98308
  117.8 1.1 copy-start.4
  118.2 1.1 copy-start.6
  120.7 10.8 %all-to-all-start.2 = ((bf16[32,4,4,128]{3,1,2,0:T(4,128)(2,1)}), bf16[32,4,4,128]{3,1,2,0:T(4,128)(2,1)S(1)}, u32[]{:S(2)}, u32[]{:S(2)}) async-start(bf16[32,4,4,128]{3,1,2,0:T(4,128)(2,1)} %copy.97), calls=%async_computation.2 | async-start | bytes 262144 | tf_op jit(solution)/shard_map/all_to_all | solution.py:160
  123.4 49.5 %copy-start.8 = (bf16[128,128]{1,0:T(8,128)(2,1)S(1)}, bf16[128,128]{1,0:T(8,128)(2,1)}, u32[]{:S(2)}) copy-start(bf16[128,128]{1,0:T(8,128)(2,1)} %param.27) | copy-start | bytes 98308
  131.5 10.8 %all-to-all-start.1 = ((bf16[32,4,4,128]{3,1,2,0:T(4,128)(2,1)}), bf16[32,4,4,128]{3,1,2,0:T(4,128)(2,1)S(1)}, u32[]{:S(2)}, u32[]{:S(2)}) async-start(bf16[32,4,4,128]{3,1,2,0:T(4,128)(2,1)} %copy.94), calls=%async_computation.1 | async-start | bytes 262144 | tf_op jit(solution)/shard_map/all_to_all | solution.py:159
  161.7 10.8 %all-to-all-start.3 = ((bf16[32,1,4,4,128]{4,3,2,1,0:T(4,128)(2,1)}), bf16[32,1,4,4,128]{4,3,2,1,0:T(4,128)(2,1)S(1)}, u32[]{:S(2)}, u32[]{:S(2)}) async-start(bf16[32,1,4,4,128]{4,3,2,1,0:T(4,128)(2,1)} %constant_dynamic-update-slice_fusion), calls=%async_computation.3 | async-start | bytes 262144 | tf_op jit(solution)/shard_map/all_to_all | solution.py:164
